TPU v7x, 32 devices: a whole 2x2x4 slice. The times are simulated.
32 devices in a mesh: freq: 4 (over y, core), stcol: 8 (over z, x).
Axes of the slice: x: 2, y: 2, z: 4, core: 2. Of those that a mesh axis runs over, the one named last changes fastest.
Arguments:
- visibilities: float32 [2, 4, 512, 1, 512], P(None, 'freq', 'stcol'), may hold values from -28.8 to 28.8
- positions: float32 [3, 1, 512], replicated, may hold values from -3 to 3
- source_lmn: float32 [3, 1024], replicated, may hold values from -0.5 to 0.5
- source_flux: float32 [1024], replicated, may hold values from 0.02 to 0.2
- cluster_map: int32 [1024], replicated, may hold values from 0 to 15, as said below
- station_order: int32 [512], replicated, may hold values from 0 to 511, each once
- penalty: float32 [16], replicated, may hold values from 9.8304 to 196.608
- offsets: float32 [2, 4, 16, 512], P(None, 'freq'), may hold values from -1.2 to 1.2
Outputs:
- gains: float32 [2, 4, 16, 512], P(None, 'freq', None, 'stcol')
- consensus: float32 [2, 4, 16, 512], P(None, 'freq', None, 'stcol')
Inputs may be any that keep to these rules, and one draw needn't show every extreme that they name: `cluster_map`: each of the 16 directions is named by exactly 64 sources. `station_order`: every station stands exactly once.
All inputs are finite; a program needn't handle non-finite values.
Results may differ from a plain program's by a relative error of at most 0.00011.
Values sent between devices are 32-bit elements; how exact they have to be, the bound alone decides.
A program may use at most 64 MiB of HBM per device.

v0:
```python
import math
import jax
import jax.numpy as jnp
from jax import lax
from jax.sharding import PartitionSpec as P

ADMM = 2
PASSES = 2
HIGHEST = lax.Precision.HIGHEST


def frequencies(channels):
    return 1.0 + 0.5 * jnp.arange(channels, dtype=jnp.float32) / channels


def basis_table(channels):
    centre = (jnp.arange(channels, dtype=jnp.float32) - 0.5 * (channels - 1)) / channels
    columns = [jnp.ones_like(centre), centre, centre * centre]
    finished = []
    for column in columns:
        for before in finished:
            column = column - jnp.sum(column * before) * before
        finished.append(column / jnp.sqrt(jnp.sum(column * column)))
    return jnp.stack(finished, axis=1)


def group_sources(source_lmn, source_flux, cluster_map, directions):
    ranking = jnp.argsort(cluster_map, stable=True)
    cosines = jnp.take(source_lmn, ranking, axis=1).reshape(3, directions, -1)
    brightness = jnp.take(source_flux, ranking).reshape(directions, -1)
    return (jnp.moveaxis(cosines, 1, 0), brightness)


def contract(row_part, column_part):
    return jnp.einsum("ctps,ctjs->cjtp", row_part, column_part, precision=HIGHEST)


def model_block(positions, direction_cosines, weights, freq_scale, column_ids):
    projected = (
        positions[0][:, :, None] * direction_cosines[0]
        + positions[1][:, :, None] * direction_cosines[1]
    )
    projected = projected + positions[2][:, :, None] * direction_cosines[2]
    phases = 2.0 * math.pi * freq_scale[:, None, None, None] * projected[None]
    cosine = jnp.cos(phases)
    sine_part = jnp.sin(phases)
    weighted_cos = cosine * weights
    weighted_sin = sine_part * weights
    column_cos = jnp.take(cosine, column_ids, axis=2)
    column_sin = jnp.take(sine_part, column_ids, axis=2)
    model_real = contract(weighted_cos, column_cos) + contract(weighted_sin, column_sin)
    model_imag = contract(weighted_sin, column_cos) - contract(weighted_cos, column_sin)
    station_ids = jnp.arange(positions.shape[2], dtype=jnp.int32)
    retained = (column_ids[:, None] != station_ids[None, :]).astype(model_real.dtype)
    retained = retained[None, :, None, :]
    return (model_real * retained, model_imag * retained)


def build_models(positions, cosines, brightness, freq_scale, column_ids):

    def one_model(entry):
        return model_block(positions, entry[0], entry[1], freq_scale, column_ids)

    return lax.map(one_model, (cosines, brightness))


def gain_update(numerator, denominator, gains, consensus, multiplier, penalty):
    weight_pen = penalty[:, None]
    scaling = 1.0 / (denominator + weight_pen)
    fresh = (numerator + gains * denominator + weight_pen * (consensus - multiplier)) * scaling
    return 0.5 * (gains + fresh)


def pass_terms(visibilities, gains, model_real, model_imag, column_ids):
    column_gains = jnp.take(gains, column_ids, axis=3)
    column_real = jnp.moveaxis(column_gains[0], 1, 0)[:, :, :, None, None]
    column_imag = jnp.moveaxis(column_gains[1], 1, 0)[:, :, :, None, None]
    row_real = jnp.moveaxis(gains[0], 1, 0)[:, :, None, None, :]
    row_imag = jnp.moveaxis(gains[1], 1, 0)[:, :, None, None, :]
    along_real = model_real * column_real + model_imag * column_imag
    along_imag = model_imag * column_real - model_real * column_imag
    pred_real = row_real * along_real - row_imag * along_imag
    pred_imag = row_real * along_imag + row_imag * along_real
    resid_real = visibilities[0] - jnp.sum(pred_real, axis=0)
    resid_imag = visibilities[1] - jnp.sum(pred_imag, axis=0)
    num_real = jnp.sum(resid_real * along_real + resid_imag * along_imag, axis=(2, 3))
    num_imag = jnp.sum(resid_imag * along_real - resid_real * along_imag, axis=(2, 3))
    denominator = jnp.sum(along_real * along_real + along_imag * along_imag, axis=(2, 3))
    numerator = jnp.moveaxis(jnp.stack([num_real, num_imag]), 1, 2)
    return (numerator, jnp.moveaxis(denominator, 0, 1)[None])


def channel_fit(values, local_basis):
    partial_sums = jnp.einsum("fj,rfkp->rjkp", local_basis, values, precision=HIGHEST)
    coefficients = lax.psum(partial_sums, "freq")
    return jnp.einsum("fj,rjkp->rfkp", local_basis, coefficients, precision=HIGHEST)


def on_device(
    visibilities, positions, source_lmn, source_flux, cluster_map, station_order, penalty, offsets
):
    chan_dev = visibilities.shape[1]
    column_count = visibilities.shape[2]
    stations = visibilities.shape[4]
    directions = penalty.shape[0]
    channels = chan_dev * lax.axis_size("freq")
    row_index = lax.axis_index("freq")
    col_index = lax.axis_index("stcol")
    owned_count = stations // lax.axis_size("stcol")
    column_ids = lax.dynamic_slice_in_dim(station_order, col_index * column_count, column_count)
    freq_scale = lax.dynamic_slice_in_dim(frequencies(channels), row_index * chan_dev, chan_dev)
    basis = basis_table(channels)
    local_basis = lax.dynamic_slice_in_dim(basis, row_index * chan_dev, chan_dev, 0)
    cosines, brightness = group_sources(source_lmn, source_flux, cluster_map, directions)
    model_real, model_imag = build_models(positions, cosines, brightness, freq_scale, column_ids)
    gains = jnp.stack([1.0 + offsets[0], offsets[1]])
    consensus = gains
    multiplier = jnp.zeros_like(gains)
    for admm_step in range(ADMM):
        for sweep_index in range(PASSES):
            numerator, denominator = pass_terms(
                visibilities, gains, model_real, model_imag, column_ids
            )
            numerator, denominator = lax.psum((numerator, denominator), "stcol")
            gains = gain_update(numerator, denominator, gains, consensus, multiplier, penalty)
        consensus = channel_fit(gains + multiplier, local_basis)
        multiplier = multiplier + gains - consensus
    gains_out = lax.dynamic_slice_in_dim(gains, col_index * owned_count, owned_count, 3)
    cons_out = lax.dynamic_slice_in_dim(consensus, col_index * owned_count, owned_count, 3)
    return (gains_out, cons_out)


def solution(mesh):
    in_specs = (
        P(None, "freq", "stcol", None, None),
        P(),
        P(),
        P(),
        P(),
        P(),
        P(),
        P(None, "freq", None, None),
    )
    out_specs = (P(None, "freq", None, "stcol"), P(None, "freq", None, "stcol"))
    return jax.shard_map(
        on_device, mesh=mesh, in_specs=in_specs, out_specs=out_specs, check_vma=False
    )
```

profile of v0, /device:TPU:0, one launch (start us, length us, event | category | flops | bytes accessed | tf_op | source)
XLA Modules:
  0.0 582.2 jit_solution(7560727911189916129)
XLA Ops:
  7.3 5.1 sort.17
  16.7 2.8 gather_fusion.2
  19.9 4.5 gather_fusion.3
  25.8 137.8 %while.14 = (s32[]{:T(128)}, f32[16,1,64,1,512]{4,2,3,1,0:T(8,128)S(1)}, f32[16,1,64,1,512]{4,2,3,1,0:T(8,128)}, s32[64]{0:T(128)S(1)}, f32[1,1,1,1]{3,2,1,0:T(1...) while((s32[]{:T(128)}, ...), condition=%wide.region_2.4_spmd, body=%wide.region_1.3_spmd.sunk | while | flops 101992000 | bytes 1256825 | solution.py:64
  29.5 2.0 fusion.98
  33.0 1.4 fusion.96
  36.1 1.4 fusion.97
  38.1 2.1 fusion.98
  41.6 1.4 fusion.96
  44.7 1.4 fusion.97
  46.7 2.1 fusion.98
  50.2 1.4 fusion.96
  53.4 1.4 fusion.97
  55.4 2.1 fusion.98
  58.8 1.4 fusion.96
  62.0 1.4 fusion.97
  64.0 2.1 fusion.98
  67.4 1.4 fusion.96
  70.6 1.4 fusion.97
  72.6 2.0 fusion.98
  76.0 1.4 fusion.96
  79.2 1.4 fusion.97
  81.2 2.1 fusion.98
  84.7 1.4 fusion.96
  87.8 1.4 fusion.97
  89.8 2.1 fusion.98
  93.3 1.4 fusion.96
  96.4 1.4 fusion.97
  98.4 2.0 fusion.98
  101.9 1.4 fusion.96
  105.0 1.4 fusion.97
  107.0 2.1 fusion.98
  110.5 1.4 fusion.96
  115.7 2.0 fusion.98
  119.1 1.4 fusion.96
  124.3 2.1 fusion.98
  127.7 1.4 fusion.96
  130.9 1.4 fusion.97
  132.9 2.0 fusion.98
  136.3 1.4 fusion.96
  139.5 1.4 fusion.97
  141.5 2.1 fusion.98
  144.9 1.4 fusion.96
  150.1 2.0 fusion.98
  153.5 1.4 fusion.96
  156.7 1.4 fusion.97
  158.7 2.1 fusion.98
  162.2 1.4 fusion.96
  163.6 2.6 subtract_reduce_fusion.7
  169.5 38.9 %psum.71 = f32[1,1,16,512]{3,2,1,0:T(8,128)S(1)} all-reduce(f32[1,1,16,512]{3,2,1,0:T(8,128)S(1)} %bitcast.261), channel_id=1, replica_groups=mesh['freq'=4,'stcol'=8] {'stcol'}, use_global_device_ids=true, to_apply=%region_9.12 | all-reduce | flops 8192 | bytes 65536 | tf_op jit(solution)/shard_map/psum | solution.py:124
  214.6 25.7 %all-reduce.7.cloned.1.call-done = f32[2,1,16,512]{3,2,1,0:T(8,128)} async-done(((f32[2,1,16,512]{3,2,1,0:T(8,128)}), f32[2,1,16,512]{3,2,1,0:T(8,128)}) %all-reduce.7.cloned.1.call-update) | async-done | bytes 65552 | tf_op jit(solution)/shard_map/psum | solution.py:124
  243.5 2.6 subtract_reduce_fusion.5
  248.1 36.2 %psum.73 = f32[1,1,16,512]{3,2,1,0:T(8,128)S(1)} all-reduce(f32[1,1,16,512]{3,2,1,0:T(8,128)S(1)} %bitcast.262), channel_id=1, replica_groups=mesh['freq'=4,'stcol'=8] {'stcol'}, use_global_device_ids=true, to_apply=%region_16.19 | all-reduce | flops 8192 | bytes 65536 | tf_op jit(solution)/shard_map/psum | solution.py:124
  284.4 33.1 %all-reduce.9.cloned.1.call-done = f32[2,1,16,512]{3,2,1,0:T(8,128)} async-done(((f32[2,1,16,512]{3,2,1,0:T(8,128)}), f32[2,1,16,512]{3,2,1,0:T(8,128)}) %all-reduce.9.cloned.1.call-update) | async-done | bytes 65552 | tf_op jit(solution)/shard_map/psum | solution.py:124
  319.8 2.6 subtract_reduce_fusion.3
  323.7 36.1 %psum.75 = f32[1,1,16,512]{3,2,1,0:T(8,128)S(1)} all-reduce(f32[1,1,16,512]{3,2,1,0:T(8,128)S(1)} %bitcast.264), channel_id=1, replica_groups=mesh['freq'=4,'stcol'=8] {'stcol'}, use_global_device_ids=true, to_apply=%region_23.26 | all-reduce | flops 8192 | bytes 65536 | tf_op jit(solution)/shard_map/psum | solution.py:124
  361.4 28.7 %all-reduce.13.cloned.1.call-done = f32[2,3,16,512]{3,2,1,0:T(8,128)} async-done(((f32[2,3,16,512]{3,2,1,0:T(8,128)}), f32[2,3,16,512]{3,2,1,0:T(8,128)}) %all-reduce.13.cloned.1.call-update) | async-done | bytes 196624 | tf_op jit(solution)/shard_map/psum | solution.py:95
  390.1 1.6 fusion.59
  391.7 71.0 %all-reduce.11.cloned.1.call-done = f32[2,1,16,512]{3,2,1,0:T(8,128)} async-done(((f32[2,1,16,512]{3,2,1,0:T(8,128)}), f32[2,1,16,512]{3,2,1,0:T(8,128)}) %all-reduce.11.cloned.1.call-update) | async-done | bytes 65552 | tf_op jit(solution)/shard_map/psum | solution.py:124
  465.0 2.6 subtract_reduce_fusion.1
  469.5 36.2 %psum.78 = f32[1,1,16,512]{3,2,1,0:T(8,128)S(1)} all-reduce(f32[1,1,16,512]{3,2,1,0:T(8,128)S(1)} %bitcast.263), channel_id=1, replica_groups=mesh['freq'=4,'stcol'=8] {'stcol'}, use_global_device_ids=true, to_apply=%region_36.39 | all-reduce | flops 8192 | bytes 65536 | tf_op jit(solution)/shard_map/psum | solution.py:124
  505.8 33.1 %all-reduce.15.cloned.1.call-done = f32[2,1,16,512]{3,2,1,0:T(8,128)} async-done(((f32[2,1,16,512]{3,2,1,0:T(8,128)}), f32[2,1,16,512]{3,2,1,0:T(8,128)}) %all-reduce.15.cloned.1.call-update) | async-done | bytes 65552 | tf_op jit(solution)/shard_map/psum | solution.py:124
  541.3 31.8 %all-reduce.17.cloned.1.call-done = f32[2,3,16,512]{3,2,1,0:T(8,128)} async-done(((f32[2,3,16,512]{3,2,1,0:T(8,128)}), f32[2,3,16,512]{3,2,1,0:T(8,128)}) %all-reduce.17.cloned.1.call-update) | async-done | bytes 196624 | tf_op jit(solution)/shard_map/psum | solution.py:95
  573.1 1.6 fusion.57
  (299 shorter events, 94.1 us)
Async XLA Ops:
  7.2 12.7 %copy-start = (f32[1024]{0:T(1024)S(1)}, f32[1024]{0:T(1024)}, u32[]{:S(2)}) copy-start(f32[1024]{0:T(1024)} %param.17) | copy-start | bytes 12292
  7.2 233.1 %all-reduce.7.cloned.1.call-start = ((), (), s32[]{:S(2)}) async-start(), calls=%async_computation | async-start | bytes 131072 | tf_op jit(solution)/shard_map/psum | solution.py:124
  13.1 0.8 copy-start.7
  13.1 1.9 copy-start.6
  19.9 5.9 %copy-start.3 = (f32[3,1,512]{2,1,0:T(1,128)S(1)}, f32[3,1,512]{2,1,0:T(1,128)}, u32[]{:S(2)}) copy-start(f32[3,1,512]{2,1,0:T(1,128)} %param.15) | copy-start | bytes 18436
  19.9 5.9 %copy-start.8 = (s32[64]{0:T(128)S(1)}, s32[64]{0:T(128)}, u32[]{:S(2)}) copy-start(s32[64]{0:T(128)} %copy-done.7) | copy-start | bytes 772
  25.8 137.8 %copy-start.5 = (f32[16,64]{1,0:T(8,128)S(1)}, f32[16,64]{1,0:T(8,128)}, u32[]{:S(2)}) copy-start(f32[16,64]{1,0:T(8,128)} %copy.125) | copy-start | bytes 12292
  163.6 2.6 copy-start.1
  166.5 47.9 %copy-start.4 = (f32[16]{0:T(128)S(1)}, f32[16]{0:T(128)}, u32[]{:S(2)}) copy-start(f32[16]{0:T(128)} %param.20) | copy-start | bytes 196
  168.2 149.4 %all-reduce.9.cloned.1.call-start = ((), (), s32[]{:S(2)}) async-start(), calls=%async_computation.1 | async-start | bytes 131072 | tf_op jit(solution)/shard_map/psum | solution.py:124
  246.4 71.1 %copy-start.2 = (f32[2,1,16,512]{3,2,1,0:T(8,128)S(1)}, f32[2,1,16,512]{3,2,1,0:T(8,128)}, u32[]{:S(2)}) copy-start(f32[2,1,16,512]{3,2,1,0:T(8,128)} %all-reduce.7.cloned.1.call-done) | copy-start | bytes 196612
  248.1 142.0 %all-reduce.13.cloned.1.call-start = ((), (), s32[]{:S(2)}) async-start(), calls=%async_computation.3 | async-start | bytes 393216 | tf_op jit(solution)/shard_map/psum | solution.py:95
  360.7 102.0 %all-reduce.11.cloned.1.call-start = ((), (), s32[]{:S(2)}) async-start(), calls=%async_computation.2 | async-start | bytes 131072 | tf_op jit(solution)/shard_map/psum | solution.py:124
  361.4 177.5 %all-reduce.15.cloned.1.call-start = ((), (), s32[]{:S(2)}) async-start(), calls=%async_computation.4 | async-start | bytes 131072 | tf_op jit(solution)/shard_map/psum | solution.py:124
  469.5 103.6 %all-reduce.17.cloned.1.call-start = ((), (), s32[]{:S(2)}) async-start(), calls=%async_computation.5 | async-start | bytes 393216 | tf_op jit(solution)/shard_map/psum | solution.py:95
Sparse Core Ops, SparseCore 0:
  168.3 71.9 all-reduce.6
  248.2 69.2 all-reduce.8
  360.8 29.2 all-reduce.12
  393.4 69.2 all-reduce.10
  469.6 69.2 all-reduce.14
  541.1 31.9 all-reduce.16
where the time goes:
time: 583 us; the launch traced here: 582 us
  waiting for transfers between devices  223 us (38%)
  blocking collectives  147 us (25%)
  matrix products  103 us (18%)
  other arithmetic  52.9 us (9%)
  local copies, waits for them, and re-layouts  35.6 us (6%)
  between operations  18 us (3%)
    psum x4, waiting for transfers between devices, on_device(): numerator, denominator = lax.psum((numerator, denominator), 'stcol')  163 us
    psum x4, blocking collectives, on_device(): numerator, denominator = lax.psum((numerator, denominator), 'stcol')  147 us
    dot_general x64, matrix products, contract(): jnp.einsum('ctps,ctjs->cjtp', row_part, column_part, precision=HIGHEST)  100 us
    psum x2, waiting for transfers between devices, channel_fit(): coefficients = lax.psum(partial_sums, 'freq')  60.4 us
    another operation x16, other arithmetic, model_block(): column_sin = jnp.take(sine_part, column_ids, axis=2)  16.5 us
  transfers between devices with their start and end apart: 6, of which 6 were waited for; matrix products, arithmetic and copies ran while one was open for 1% of the time, Pallas kernels for 0%

commit v1 on v0

--- a/solution.py
+++ b/solution.py
@@ -92,7 +92,8 @@
 
 def channel_fit(values, local_basis):
     partial_sums = jnp.einsum("fj,rfkp->rjkp", local_basis, values, precision=HIGHEST)
-    coefficients = lax.psum(partial_sums, "freq")
+    parts = lax.all_gather(partial_sums, "freq")
+    coefficients = jnp.sum(parts, axis=0)
     return jnp.einsum("fj,rjkp->rfkp", local_basis, coefficients, precision=HIGHEST)
 
 

time: 583 us -> 488 us (0.84)
  waiting for transfers between devices: 223 us -> 116 us
  blocking collectives: 147 us -> 165 us
    psum x2 -> x0, waiting for transfers between devices: 60.4 us -> none  [channel_fit(): coefficients = lax.psum(partial_sums, 'freq')]
    psum x4, waiting for transfers between devices: 163 us -> 116 us  [on_device(): numerator, denominator = lax.psum((numerator, denominator), 'stcol')]
    all_gather x0 -> x2, blocking collectives: none -> 17.1 us  [channel_fit(): parts = lax.all_gather(partial_sums, 'freq')]
  transfers between devices with their start and end apart: 6 -> 4, of which waited for: 6 -> 4; matrix products, arithmetic and copies ran while one was open for 1% -> 1% of each run, Pallas kernels for 0% -> 0%
where the time goes in v1:
time: 488 us; the launch traced here: 487 us
  blocking collectives  165 us (34%)
  waiting for transfers between devices  116 us (24%)
  matrix products  102 us (21%)
  other arithmetic  51.4 us (11%)
  local copies, waits for them, and re-layouts  34.6 us (7%)
  between operations  17.6 us (4%)
    psum x4, blocking collectives, on_device(): numerator, denominator = lax.psum((numerator, denominator), 'stcol')  147 us
    psum x4, waiting for transfers between devices, on_device(): numerator, denominator = lax.psum((numerator, denominator), 'stcol')  116 us
    dot_general x64, matrix products, contract(): jnp.einsum('ctps,ctjs->cjtp', row_part, column_part, precision=HIGHEST)  100 us
    all_gather x2, blocking collectives, channel_fit(): parts = lax.all_gather(partial_sums, 'freq')  17.1 us
    another operation x16, other arithmetic, model_block(): column_sin = jnp.take(sine_part, column_ids, axis=2)  16.5 us
    reduce_sum x4, other arithmetic, pass_terms(): resid_real = visibilities[0] - jnp.sum(pred_real, axis=0)  10.2 us
  transfers between devices with their start and end apart: 4, of which 4 were waited for; matrix products, arithmetic and copies ran while one was open for 1% of the time, Pallas kernels for 0%

profile of v1, /device:TPU:0, one launch (start us, length us, event | category | flops | bytes accessed | tf_op | source)
XLA Modules:
  0.0 487.1 jit_solution(12452180796771630538)
XLA Ops:
  7.3 5.1 %sort.17 = (s32[1024]{0:T(1024)}, s32[1024]{0:T(1024)S(1)}) sort(s32[1024]{0:T(1024)} %param.18, s32[1024]{0:T(1024)S(1)} %iota.29), dimensions={0}, to_apply=%region_0.0 | sort | flops 10240 | bytes 16384 | tf_op jit(solution)/shard_map/jit(argsort)/sort | solution.py:28
  16.1 2.8 gather_fusion.2
  19.2 4.5 gather_fusion.3
  25.1 137.8 %while.14 = (s32[]{:T(128)}, f32[16,1,64,1,512]{4,2,3,1,0:T(8,128)S(1)}, f32[16,1,64,1,512]{4,2,3,1,0:T(8,128)}, s32[64]{0:T(128)S(1)}, f32[1,1,1,1]{3,2,1,0:T(1...) while((s32[]{:T(128)}, ...), condition=%wide.region_2.4_spmd, body=%wide.region_1.3_spmd.sunk | while | flops 101992000 | bytes 1256825 | solution.py:64
  26.9 1.4 fusion.97
  28.9 2.0 fusion.98
  32.3 1.4 fusion.96
  35.5 1.4 fusion.97
  37.5 2.1 fusion.98
  40.9 1.4 fusion.96
  44.1 1.4 fusion.97
  46.1 2.1 fusion.98
  49.6 1.4 fusion.96
  52.7 1.4 fusion.97
  54.7 2.1 fusion.98
  58.2 1.4 fusion.96
  61.3 1.4 fusion.97
  63.3 2.1 fusion.98
  66.8 1.4 fusion.96
  69.9 1.4 fusion.97
  72.0 2.0 fusion.98
  75.4 1.4 fusion.96
  78.5 1.4 fusion.97
  80.6 2.1 fusion.98
  84.0 1.4 fusion.96
  87.2 1.4 fusion.97
  89.2 2.1 fusion.98
  92.6 1.4 fusion.96
  95.8 1.4 fusion.97
  97.8 2.0 fusion.98
  101.2 1.4 fusion.96
  104.4 1.4 fusion.97
  106.4 2.1 fusion.98
  109.9 1.4 fusion.96
  115.0 2.0 fusion.98
  118.5 1.4 fusion.96
  123.6 2.1 fusion.98
  127.1 1.4 fusion.96
  130.2 1.4 fusion.97
  132.2 2.0 fusion.98
  135.7 1.4 fusion.96
  138.8 1.4 fusion.97
  140.9 2.1 fusion.98
  144.3 1.4 fusion.96
  147.5 1.4 fusion.97
  149.5 2.0 fusion.98
  152.9 1.4 fusion.96
  156.1 1.4 fusion.97
  158.1 2.1 fusion.98
  161.5 1.4 fusion.96
  163.0 2.6 subtract_reduce_fusion.7
  168.8 38.9 %psum.57 = f32[1,1,16,512]{3,2,1,0:T(8,128)S(1)} all-reduce(f32[1,1,16,512]{3,2,1,0:T(8,128)S(1)} %bitcast.265), channel_id=1, replica_groups=mesh['freq'=4,'stcol'=8] {'stcol'}, use_global_device_ids=true, to_apply=%region_9.12 | all-reduce | flops 8192 | bytes 65536 | tf_op jit(solution)/shard_map/psum | solution.py:125
  213.7 26.0 %all-reduce.5.cloned.1.call-done = f32[2,1,16,512]{3,2,1,0:T(8,128)} async-done(((f32[2,1,16,512]{3,2,1,0:T(8,128)}), f32[2,1,16,512]{3,2,1,0:T(8,128)}) %all-reduce.5.cloned.1.call-update) | async-done | bytes 65552 | tf_op jit(solution)/shard_map/psum | solution.py:125
  242.8 2.5 subtract_reduce_fusion.5
  247.3 36.2 %psum.59 = f32[1,1,16,512]{3,2,1,0:T(8,128)S(1)} all-reduce(f32[1,1,16,512]{3,2,1,0:T(8,128)S(1)} %bitcast.266), channel_id=1, replica_groups=mesh['freq'=4,'stcol'=8] {'stcol'}, use_global_device_ids=true, to_apply=%region_16.19 | all-reduce | flops 8192 | bytes 65536 | tf_op jit(solution)/shard_map/psum | solution.py:125
  283.6 33.1 %all-reduce.7.cloned.1.call-done = f32[2,1,16,512]{3,2,1,0:T(8,128)} async-done(((f32[2,1,16,512]{3,2,1,0:T(8,128)}), f32[2,1,16,512]{3,2,1,0:T(8,128)}) %all-reduce.7.cloned.1.call-update) | async-done | bytes 65552 | tf_op jit(solution)/shard_map/psum | solution.py:125
  318.9 2.5 subtract_reduce_fusion.3
  323.5 36.2 %psum.61 = f32[1,1,16,512]{3,2,1,0:T(8,128)S(1)} all-reduce(f32[1,1,16,512]{3,2,1,0:T(8,128)S(1)} %bitcast.267), channel_id=1, replica_groups=mesh['freq'=4,'stcol'=8] {'stcol'}, use_global_device_ids=true, to_apply=%region_23.26 | all-reduce | flops 8192 | bytes 65536 | tf_op jit(solution)/shard_map/psum | solution.py:125
  359.7 8.6 %all-gather = f32[8,3,16,512]{3,2,1,0:T(8,128)S(1)} all-gather(f32[2,3,16,512]{3,2,1,0:T(8,128)S(1)} %multiply_bitcast_fusion.1), channel_id=2, replica_groups=mesh['freq'=4,'stcol'=8] {'freq'}, dimensions={0}, use_global_device_ids=true | all-gather | bytes 983040 | tf_op jit(solution)/shard_map/all_gather | solution.py:95
  369.1 23.8 %all-reduce.9.cloned.1.call-done = f32[2,1,16,512]{3,2,1,0:T(8,128)} async-done(((f32[2,1,16,512]{3,2,1,0:T(8,128)}), f32[2,1,16,512]{3,2,1,0:T(8,128)}) %all-reduce.9.cloned.1.call-update) | async-done | bytes 65552 | tf_op jit(solution)/shard_map/psum | solution.py:125
  395.0 2.5 subtract_reduce_fusion.1
  399.5 36.2 %psum.63 = f32[1,1,16,512]{3,2,1,0:T(8,128)S(1)} all-reduce(f32[1,1,16,512]{3,2,1,0:T(8,128)S(1)} %bitcast.268), channel_id=1, replica_groups=mesh['freq'=4,'stcol'=8] {'stcol'}, use_global_device_ids=true, to_apply=%region_36.39 | all-reduce | flops 8192 | bytes 65536 | tf_op jit(solution)/shard_map/psum | solution.py:125
  435.8 33.1 %all-reduce.11.cloned.1.call-done = f32[2,1,16,512]{3,2,1,0:T(8,128)} async-done(((f32[2,1,16,512]{3,2,1,0:T(8,128)}), f32[2,1,16,512]{3,2,1,0:T(8,128)}) %all-reduce.11.cloned.1.call-update) | async-done | bytes 65552 | tf_op jit(solution)/shard_map/psum | solution.py:125
  469.9 8.6 %all-gather.1 = f32[8,3,16,512]{3,2,1,0:T(8,128)S(1)} all-gather(f32[2,3,16,512]{3,2,1,0:T(8,128)S(1)} %multiply_bitcast_fusion), channel_id=3, replica_groups=mesh['freq'=4,'stcol'=8] {'freq'}, dimensions={0}, use_global_device_ids=true | all-gather | bytes 983040 | tf_op jit(solution)/shard_map/all_gather | solution.py:95
  (289 shorter events, 90.1 us)
Async XLA Ops:
  7.2 12.1 %copy-start = (f32[1024]{0:T(1024)S(1)}, f32[1024]{0:T(1024)}, u32[]{:S(2)}) copy-start(f32[1024]{0:T(1024)} %param.17) | copy-start | bytes 12292
  7.2 232.5 %all-reduce.5.cloned.1.call-start = ((), (), s32[]{:S(2)}) async-start(), calls=%async_computation | async-start | bytes 131072 | tf_op jit(solution)/shard_map/psum | solution.py:125
  19.2 5.9 %copy-start.3 = (f32[3,1,512]{2,1,0:T(1,128)S(1)}, f32[3,1,512]{2,1,0:T(1,128)}, u32[]{:S(2)}) copy-start(f32[3,1,512]{2,1,0:T(1,128)} %param.15) | copy-start | bytes 18436
  162.9 2.6 copy-start.1
  165.9 47.6 %copy-start.4 = (f32[16]{0:T(128)S(1)}, f32[16]{0:T(128)}, u32[]{:S(2)}) copy-start(f32[16]{0:T(128)} %param.20) | copy-start | bytes 196
  167.5 149.2 %all-reduce.7.cloned.1.call-start = ((), (), s32[]{:S(2)}) async-start(), calls=%async_computation.1 | async-start | bytes 131072 | tf_op jit(solution)/shard_map/psum | solution.py:125
  245.6 71.1 %copy-start.2 = (f32[2,1,16,512]{3,2,1,0:T(8,128)S(1)}, f32[2,1,16,512]{3,2,1,0:T(8,128)}, u32[]{:S(2)}) copy-start(f32[2,1,16,512]{3,2,1,0:T(8,128)} %all-reduce.5.cloned.1.call-done) | copy-start | bytes 196612
  247.3 145.6 %all-reduce.9.cloned.1.call-start = ((), (), s32[]{:S(2)}) async-start(), calls=%async_computation.2 | async-start | bytes 131072 | tf_op jit(solution)/shard_map/psum | solution.py:125
  323.4 145.5 %all-reduce.11.cloned.1.call-start = ((), (), s32[]{:S(2)}) async-start(), calls=%async_computation.3 | async-start | bytes 131072 | tf_op jit(solution)/shard_map/psum | solution.py:125
Sparse Core Ops, SparseCore 0:
  167.6 71.9 all-reduce.4
  247.4 69.2 all-reduce.6
  323.5 69.2 all-reduce.8
  399.6 69.2 all-reduce.10
